TPU v7x, 512 devices: a whole 4x8x8 slice. The times are simulated.
512 devices in a mesh: ctx: 64 (over z_lo, y, core), tp: 8 (over z_hi, x).
Axes of the slice: x: 4, y: 8, z: 8 (z_hi: 2, z_lo: 4; z = z_hi * 4 + z_lo), core: 2. Of those that a mesh axis runs over, the one named last changes fastest.
Arguments:
- hidden_in: bfloat16 [16384, 2048], P('ctx', 'tp'), may hold values from -6 to 6
- ln_gain: float32 [2048], replicated, may hold values from 0.1 to 1.9
- ln_bias: float32 [2048], replicated, may hold values from -3 to 3
- w_qkv: bfloat16 [3, 2048, 2048], P(None, None, 'tp')
- w_out: bfloat16 [2048, 2048], P('tp'), may hold values from -0.375 to 0.375
- segment_ids: int32 [16384], P('ctx'), may hold values from 0 to 2, as said below
- prompt_lengths: int32 [3], replicated, may hold values from 1 to 8192, as said below
- page_table: int32 [3, 64], replicated, may hold values from -1 to 319, as said below
Outputs:
- attn_out: bfloat16 [16384, 2048], P('ctx', 'tp')
- kv_cache: bfloat16 [320, 128, 2, 2048], P('ctx', None, None, 'tp')
Inputs may be any that keep to these rules, and one draw needn't show every extreme that they name: `segment_ids`: each prompt's tokens are consecutive and the numbers never fall along the tokens; prompt i holds exactly prompt_lengths[i] tokens. `prompt_lengths`: the lengths sum to 16384; prompt 0 is shorter than 256 tokens and not a multiple of 128; prompt 1 is the longest, exactly 8192 tokens. `page_table`: for page j of prompt i with j * 128 below prompt_lengths[i], the entry is owner * 5 + slot with slot below 5, where owner is the ctx index whose tokens include the page's first token, starts_i + j * 128; distinct pages have distinct entries; all other entries are -1.
All inputs are finite; a program needn't handle non-finite values.
Results may differ from a plain program's by a relative error of at most 0.013.
Values may be sent and summed in bfloat16 or wider, within the bound.
A program may use at most 128 MiB of HBM per device.

v0:
```python
import math
import jax
import jax.numpy as jnp
from jax import lax
from jax.sharding import PartitionSpec as P

HD = 256
PAGE = 128
EPSILON = 1e-05


def passed_along(value, axis, steps):
    count = lax.axis_size(axis)
    first, last = (max(0, -steps), min(count, count - steps))
    return lax.ppermute(value, axis, [(source, source + steps) for source in range(first, last)])


def normalize(inputs, norm_gain, norm_bias):
    average = jnp.sum(inputs, axis=-1, keepdims=True) / inputs.shape[-1]
    centered = inputs - average
    spread = jnp.sum(centered * centered, axis=-1, keepdims=True) / inputs.shape[-1]
    return centered * lax.rsqrt(spread + EPSILON) * norm_gain + norm_bias


def rotary(inputs, positions):
    quarter = inputs.shape[-1] // 4
    halfway = quarter // 2
    exponent = jnp.arange(0, quarter, 2).astype(jnp.float32) / quarter
    inverse = jnp.power(jnp.float32(10000.0), -exponent)
    angles = positions.astype(jnp.float32)[:, None] * inverse[None, :]
    cosine_table = jnp.concatenate([jnp.cos(angles), jnp.cos(angles)], axis=-1)[:, None, :]
    sine_table = jnp.concatenate([jnp.sin(angles), jnp.sin(angles)], axis=-1)[:, None, :]
    leading = inputs[..., :quarter]
    turned = jnp.concatenate([-leading[..., halfway:], leading[..., :halfway]], axis=-1)
    return jnp.concatenate(
        [leading * cosine_table + turned * sine_table, inputs[..., quarter:]], axis=-1
    )


def segment_positions(segment_rows, row_index, starts):
    table_span = starts.shape[0]
    matches = segment_rows[:, None] == jnp.arange(table_span, dtype=jnp.int32)[None, :]
    first_rows = jnp.sum(jnp.where(matches, starts[None, :], 0), axis=1)
    return row_index - first_rows


def attend(carry_state, query_heads, pair_block, key_marks, query_marks, causal):
    running_max, running_sum, running_acc = carry_state
    scores = jnp.einsum(
        "qhd,khd->hqk", query_heads, pair_block[:, 0], preferred_element_type=jnp.float32
    ) / math.sqrt(query_heads.shape[-1])
    visible = query_marks[:, None] == key_marks[None, :]
    if causal:
        row_count = query_heads.shape[0]
        visible = visible & (jnp.arange(row_count)[None, :] <= jnp.arange(row_count)[:, None])
    scores = jnp.where(visible[None], scores, -jnp.inf)
    newest_max = jnp.maximum(running_max, jnp.max(scores, axis=-1))
    rescale = jnp.exp(running_max - newest_max)
    weights = jnp.exp(scores - newest_max[..., None]).astype(jnp.bfloat16)
    weights = lax.optimization_barrier(weights)
    running_sum = running_sum * rescale + jnp.sum(weights.astype(jnp.float32), axis=-1)
    running_acc = running_acc * rescale[..., None] + jnp.einsum(
        "hqk,khd->hqd", weights, pair_block[:, 1], preferred_element_type=jnp.float32
    )
    return (newest_max, running_sum, running_acc)


def visit_block(carry_state, query_heads, query_marks, pair_block, key_marks):
    tail_mark = key_marks[key_marks.shape[0] - 1]
    relevant = tail_mark == query_marks[0]
    return lax.cond(
        relevant,
        lambda current: attend(current, query_heads, pair_block, key_marks, query_marks, False),
        lambda current: current,
        carry_state,
    )


def per_device(hidden_in, ln_gain, ln_bias, w_qkv, w_out, segment_ids, prompt_lengths, page_table):
    token_rows = hidden_in.shape[0]
    model_width = w_out.shape[1]
    local_heads = w_out.shape[0] // HD
    my_index = lax.axis_index("ctx")
    reach = lax.axis_size("ctx") // 2
    whole_rows = lax.all_gather(hidden_in, "tp", axis=1, tiled=True)
    normed = normalize(whole_rows.astype(jnp.float32), ln_gain, ln_bias).astype(jnp.bfloat16)
    projected = jnp.einsum("td,jdh->tjh", normed, w_qkv, preferred_element_type=jnp.float32)
    starts = jnp.cumsum(prompt_lengths) - prompt_lengths
    row_index = my_index * token_rows + jnp.arange(token_rows, dtype=jnp.int32)
    positions = segment_positions(segment_ids, row_index, starts)
    query_heads = rotary(projected[:, 0].reshape(token_rows, local_heads, HD), positions).astype(
        jnp.bfloat16
    )
    key_heads = rotary(projected[:, 1].reshape(token_rows, local_heads, HD), positions).astype(
        jnp.bfloat16
    )
    value_heads = projected[:, 2].reshape(token_rows, local_heads, HD).astype(jnp.bfloat16)
    pair_block = jnp.stack([key_heads, value_heads], axis=1)
    own_marks = segment_ids + 1
    carry_state = (
        jnp.full((local_heads, token_rows), -jnp.inf, jnp.float32),
        jnp.zeros((local_heads, token_rows), jnp.float32),
        jnp.zeros((local_heads, token_rows, HD), jnp.float32),
    )
    carry_state = attend(carry_state, query_heads, pair_block, own_marks, own_marks, True)

    def relay_step(step, state):
        moving_pair, moving_marks, current = state
        moving_pair, moving_marks = passed_along((moving_pair, moving_marks), "ctx", 1)
        current = visit_block(current, query_heads, own_marks, moving_pair, moving_marks)
        return (moving_pair, moving_marks, current)

    carry_state = lax.fori_loop(0, reach, relay_step, (pair_block, own_marks, carry_state))[2]
    running_max, running_sum, running_acc = carry_state
    attended = (running_acc / running_sum[..., None]).astype(jnp.bfloat16)
    partial_value = jnp.einsum(
        "hqd,hde->qe",
        attended,
        w_out.reshape(local_heads, HD, model_width),
        preferred_element_type=jnp.float32,
    )
    attn_out = lax.psum_scatter(
        partial_value.astype(jnp.bfloat16), "tp", scatter_dimension=1, tiled=True
    )
    tail_pair, tail_marks = passed_along((pair_block[:PAGE], own_marks[:PAGE]), "ctx", -1)
    every_pair = jnp.concatenate([pair_block, tail_pair], axis=0)
    every_marks = jnp.concatenate([own_marks, tail_marks], axis=0)
    every_index = my_index * token_rows + jnp.arange(token_rows + PAGE, dtype=jnp.int32)
    every_segment = jnp.maximum(every_marks - 1, 0)
    every_position = segment_positions(every_segment, every_index, starts)
    page_number = every_position // PAGE
    page_offset = every_position % PAGE
    page_owner = (every_index - page_offset) // token_rows
    is_owned = (every_marks > 0) & (page_owner == my_index)
    page_count = page_table.shape[1]
    table_entry = jnp.take(
        page_table.reshape(-1),
        every_segment * page_count + jnp.clip(page_number, 0, page_count - 1),
    )
    kv_slots = token_rows // PAGE + 3
    target = jnp.where(is_owned, table_entry % kv_slots * PAGE + page_offset, -1)
    placing = (jnp.arange(kv_slots * PAGE, dtype=jnp.int32)[:, None] == target[None, :]).astype(
        jnp.bfloat16
    )
    flat_pair = every_pair.reshape(token_rows + PAGE, 2 * local_heads * HD)
    written = jnp.dot(placing, flat_pair, preferred_element_type=jnp.float32).astype(jnp.bfloat16)
    kv_cache = written.reshape(kv_slots, PAGE, 2, local_heads * HD)
    return (attn_out, kv_cache)


def solution(mesh):
    return jax.shard_map(
        per_device,
        mesh=mesh,
        in_specs=(P("ctx", "tp"), P(), P(), P(None, None, "tp"), P("tp", None), P("ctx"), P(), P()),
        out_specs=(P("ctx", "tp"), P("ctx", None, None, "tp")),
        check_vma=False,
    )
```

profile of v0, /device:TPU:8, one launch (start us, length us, event | category | flops | bytes accessed | tf_op | source)
XLA Modules:
  0.0 715.6 jit_solution(10139987149686012293)
XLA Ops:
  12.5 70.7 %all-gather.2.cloned.1.call-done = bf16[256,2048]{1,0:T(8,128)(2,1)} async-done(((bf16[256,256]{1,0:T(8,128)(2,1)}), bf16[256,2048]{1,0:T(8,128)(2,1)}) %all-gather.2.cloned.1.call-update) | async-done | bytes 1048592 | tf_op jit(solution)/shard_map/all_gather | solution.py:85
  95.2 446.7 %while.18 = (s32[]{:T(128)}, bf16[256,2,1,256]{3,0,2,1:T(8,128)(2,1)}, s32[256]{0:T(256)}, f32[1,256]{1,0:T(1,128)S(1)}, f32[1,256]{1,0:T(1,128)S(1)}, /*index=5...) while((s32[]{:T(128)}, bf16[256,2,1,256]{3,0,2,1:T(8,128)(2,1)}, ...), condition=%wide.region_11.12_spmd, body=%wide.region_6.11_spmd.sunk | while | flops 67764736 | bytes 3431739 | solution.py:113
  150.4 8.2 %collective-permute-start.1 = (s32[256]{0:T(256)}, s32[256]{0:T(256)S(1)}, u32[]{:S(2)}, u32[]{:S(2)}) collective-permute-start(s32[256]{0:T(256)} %get-tuple-element.206), channel_id=1, source_target_pairs={{0,8},{8,16},{16,24},{24,32},{32,40},{40,48},{48,56},{56,64},{64,7... | collective-permute-start | bytes 3080 | tf_op jit(solution)/shard_map/while/body/eval_jaxpr/ppermute | solution.py:15
  165.3 5.5 collective-permute-start.1
  175.1 5.7 collective-permute-start
  180.8 5.6 collective-permute-start.1
  193.2 8.8 %collective-permute-start.1 = (s32[256]{0:T(256)}, s32[256]{0:T(256)S(1)}, u32[]{:S(2)}, u32[]{:S(2)}) collective-permute-start(s32[256]{0:T(256)} %get-tuple-element.206), channel_id=1, source_target_pairs={{0,8},{8,16},{16,24},{24,32},{32,40},{40,48},{48,56},{56,64},{64,7... | collective-permute-start | bytes 3080 | tf_op jit(solution)/shard_map/while/body/eval_jaxpr/ppermute | solution.py:15
  218.5 5.6 collective-permute-start
  224.1 5.7 collective-permute-start.1
  236.6 8.8 %collective-permute-start.1 = (s32[256]{0:T(256)}, s32[256]{0:T(256)S(1)}, u32[]{:S(2)}, u32[]{:S(2)}) collective-permute-start(s32[256]{0:T(256)} %get-tuple-element.206), channel_id=1, source_target_pairs={{0,8},{8,16},{16,24},{24,32},{32,40},{40,48},{48,56},{56,64},{64,7... | collective-permute-start | bytes 3080 | tf_op jit(solution)/shard_map/while/body/eval_jaxpr/ppermute | solution.py:15
  252.2 5.5 collective-permute-start.1
  264.5 5.5 collective-permute-start.1
  276.8 5.5 collective-permute-start.1
  289.2 5.5 collective-permute-start.1
  303.2 6.8 collective-permute-start.1
  316.8 9.7 %collective-permute-start.1 = (s32[256]{0:T(256)}, s32[256]{0:T(256)S(1)}, u32[]{:S(2)}, u32[]{:S(2)}) collective-permute-start(s32[256]{0:T(256)} %get-tuple-element.206), channel_id=1, source_target_pairs={{0,8},{8,16},{16,24},{24,32},{32,40},{40,48},{48,56},{56,64},{64,7... | collective-permute-start | bytes 3080 | tf_op jit(solution)/shard_map/while/body/eval_jaxpr/ppermute | solution.py:15
  333.2 6.4 collective-permute-start.1
  349.2 6.9 collective-permute-start.1
  362.9 9.7 %collective-permute-start.1 = (s32[256]{0:T(256)}, s32[256]{0:T(256)S(1)}, u32[]{:S(2)}, u32[]{:S(2)}) collective-permute-start(s32[256]{0:T(256)} %get-tuple-element.206), channel_id=1, source_target_pairs={{0,8},{8,16},{16,24},{24,32},{32,40},{40,48},{48,56},{56,64},{64,7... | collective-permute-start | bytes 3080 | tf_op jit(solution)/shard_map/while/body/eval_jaxpr/ppermute | solution.py:15
  379.3 6.4 collective-permute-start.1
  395.2 7.0 collective-permute-start.1
  409.0 9.7 %collective-permute-start.1 = (s32[256]{0:T(256)}, s32[256]{0:T(256)S(1)}, u32[]{:S(2)}, u32[]{:S(2)}) collective-permute-start(s32[256]{0:T(256)} %get-tuple-element.206), channel_id=1, source_target_pairs={{0,8},{8,16},{16,24},{24,32},{32,40},{40,48},{48,56},{56,64},{64,7... | collective-permute-start | bytes 3080 | tf_op jit(solution)/shard_map/while/body/eval_jaxpr/ppermute | solution.py:15
  425.4 6.4 collective-permute-start.1
  438.7 6.4 collective-permute-start.1
  451.9 6.4 collective-permute-start.1
  465.1 6.4 collective-permute-start.1
  478.4 6.4 collective-permute-start.1
  491.6 6.4 collective-permute-start.1
  504.8 6.4 collective-permute-start.1
  518.0 6.4 collective-permute-start.1
  531.3 6.4 collective-permute-start.1
  565.8 143.0 %reduce-scatter.2.cloned.1.call-done = bf16[256,256]{1,0:T(8,128)(2,1)} async-done(((bf16[256,2048]{1,0:T(8,128)(2,1)}), bf16[256,256]{1,0:T(8,128)(2,1)}) %reduce-scatter.2.cloned.1.call-update) | async-done | bytes 131088 | tf_op jit(solution)/shard_map/reduce_scatter | solution.py:122
  (345 shorter events, 257.0 us)
Async XLA Ops:
  7.2 75.9 %all-gather.2.cloned.1.call-start = ((), (), s32[]{:S(2)}) async-start(), calls=%async_computation.1 | async-start | bytes 1179648 | tf_op jit(solution)/shard_map/all_gather | solution.py:85
  7.9 700.9 %reduce-scatter.2.cloned.1.call-start = ((), (), s32[]{:S(2)}) async-start(), calls=%async_computation.2 | async-start | bytes 1179648 | tf_op jit(solution)/shard_map/reduce_scatter | solution.py:122
  135.0 12.1 %collective-permute-start = (bf16[256,2,1,256]{3,0,2,1:T(8,128)(2,1)}, bf16[256,2,1,256]{3,0,2,1:T(8,128)(2,1)S(1)}, u32[]{:S(2)}, u32[]{:S(2)}) collective-permute-start(bf16[256,2,1,256]{3,0,2,1:T(8,128)(2,1)} %get-tuple-element.205), channel_id=1, source_target_pairs={{0,8},{8,16},{16,24},{24,32},{32,40},{40,48},{48,56},{56,64},{64,7... | collective-permute-start | bytes 786440 | tf_op jit(solution)/shard_map/while/body/eval_jaxpr/ppermute | solution.py:15
  147.8 14.2 %collective-permute-start = (bf16[256,2,1,256]{3,0,2,1:T(8,128)(2,1)}, bf16[256,2,1,256]{3,0,2,1:T(8,128)(2,1)S(1)}, u32[]{:S(2)}, u32[]{:S(2)}) collective-permute-start(bf16[256,2,1,256]{3,0,2,1:T(8,128)(2,1)} %get-tuple-element.205), channel_id=1, source_target_pairs={{0,8},{8,16},{16,24},{24,32},{32,40},{40,48},{48,56},{56,64},{64,7... | collective-permute-start | bytes 786440 | tf_op jit(solution)/shard_map/while/body/eval_jaxpr/ppermute | solution.py:15
  162.7 11.6 %collective-permute-start = (bf16[256,2,1,256]{3,0,2,1:T(8,128)(2,1)}, bf16[256,2,1,256]{3,0,2,1:T(8,128)(2,1)S(1)}, u32[]{:S(2)}, u32[]{:S(2)}) collective-permute-start(bf16[256,2,1,256]{3,0,2,1:T(8,128)(2,1)} %get-tuple-element.205), channel_id=1, source_target_pairs={{0,8},{8,16},{16,24},{24,32},{32,40},{40,48},{48,56},{56,64},{64,7... | collective-permute-start | bytes 786440 | tf_op jit(solution)/shard_map/while/body/eval_jaxpr/ppermute | solution.py:15
  175.1 14.8 %collective-permute-start = (bf16[256,2,1,256]{3,0,2,1:T(8,128)(2,1)}, bf16[256,2,1,256]{3,0,2,1:T(8,128)(2,1)S(1)}, u32[]{:S(2)}, u32[]{:S(2)}) collective-permute-start(bf16[256,2,1,256]{3,0,2,1:T(8,128)(2,1)} %get-tuple-element.205), channel_id=1, source_target_pairs={{0,8},{8,16},{16,24},{24,32},{32,40},{40,48},{48,56},{56,64},{64,7... | collective-permute-start | bytes 786440 | tf_op jit(solution)/shard_map/while/body/eval_jaxpr/ppermute | solution.py:15
  190.6 14.8 %collective-permute-start = (bf16[256,2,1,256]{3,0,2,1:T(8,128)(2,1)}, bf16[256,2,1,256]{3,0,2,1:T(8,128)(2,1)S(1)}, u32[]{:S(2)}, u32[]{:S(2)}) collective-permute-start(bf16[256,2,1,256]{3,0,2,1:T(8,128)(2,1)} %get-tuple-element.205), channel_id=1, source_target_pairs={{0,8},{8,16},{16,24},{24,32},{32,40},{40,48},{48,56},{56,64},{64,7... | collective-permute-start | bytes 786440 | tf_op jit(solution)/shard_map/while/body/eval_jaxpr/ppermute | solution.py:15
  206.2 11.6 %collective-permute-start = (bf16[256,2,1,256]{3,0,2,1:T(8,128)(2,1)}, bf16[256,2,1,256]{3,0,2,1:T(8,128)(2,1)S(1)}, u32[]{:S(2)}, u32[]{:S(2)}) collective-permute-start(bf16[256,2,1,256]{3,0,2,1:T(8,128)(2,1)} %get-tuple-element.205), channel_id=1, source_target_pairs={{0,8},{8,16},{16,24},{24,32},{32,40},{40,48},{48,56},{56,64},{64,7... | collective-permute-start | bytes 786440 | tf_op jit(solution)/shard_map/while/body/eval_jaxpr/ppermute | solution.py:15
  218.5 14.8 %collective-permute-start = (bf16[256,2,1,256]{3,0,2,1:T(8,128)(2,1)}, bf16[256,2,1,256]{3,0,2,1:T(8,128)(2,1)S(1)}, u32[]{:S(2)}, u32[]{:S(2)}) collective-permute-start(bf16[256,2,1,256]{3,0,2,1:T(8,128)(2,1)} %get-tuple-element.205), channel_id=1, source_target_pairs={{0,8},{8,16},{16,24},{24,32},{32,40},{40,48},{48,56},{56,64},{64,7... | collective-permute-start | bytes 786440 | tf_op jit(solution)/shard_map/while/body/eval_jaxpr/ppermute | solution.py:15
  234.0 14.8 %collective-permute-start = (bf16[256,2,1,256]{3,0,2,1:T(8,128)(2,1)}, bf16[256,2,1,256]{3,0,2,1:T(8,128)(2,1)S(1)}, u32[]{:S(2)}, u32[]{:S(2)}) collective-permute-start(bf16[256,2,1,256]{3,0,2,1:T(8,128)(2,1)} %get-tuple-element.205), channel_id=1, source_target_pairs={{0,8},{8,16},{16,24},{24,32},{32,40},{40,48},{48,56},{56,64},{64,7... | collective-permute-start | bytes 786440 | tf_op jit(solution)/shard_map/while/body/eval_jaxpr/ppermute | solution.py:15
  249.6 11.6 %collective-permute-start = (bf16[256,2,1,256]{3,0,2,1:T(8,128)(2,1)}, bf16[256,2,1,256]{3,0,2,1:T(8,128)(2,1)S(1)}, u32[]{:S(2)}, u32[]{:S(2)}) collective-permute-start(bf16[256,2,1,256]{3,0,2,1:T(8,128)(2,1)} %get-tuple-element.205), channel_id=1, source_target_pairs={{0,8},{8,16},{16,24},{24,32},{32,40},{40,48},{48,56},{56,64},{64,7... | collective-permute-start | bytes 786440 | tf_op jit(solution)/shard_map/while/body/eval_jaxpr/ppermute | solution.py:15
  261.9 11.6 %collective-permute-start = (bf16[256,2,1,256]{3,0,2,1:T(8,128)(2,1)}, bf16[256,2,1,256]{3,0,2,1:T(8,128)(2,1)S(1)}, u32[]{:S(2)}, u32[]{:S(2)}) collective-permute-start(bf16[256,2,1,256]{3,0,2,1:T(8,128)(2,1)} %get-tuple-element.205), channel_id=1, source_target_pairs={{0,8},{8,16},{16,24},{24,32},{32,40},{40,48},{48,56},{56,64},{64,7... | collective-permute-start | bytes 786440 | tf_op jit(solution)/shard_map/while/body/eval_jaxpr/ppermute | solution.py:15
  274.2 11.6 %collective-permute-start = (bf16[256,2,1,256]{3,0,2,1:T(8,128)(2,1)}, bf16[256,2,1,256]{3,0,2,1:T(8,128)(2,1)S(1)}, u32[]{:S(2)}, u32[]{:S(2)}) collective-permute-start(bf16[256,2,1,256]{3,0,2,1:T(8,128)(2,1)} %get-tuple-element.205), channel_id=1, source_target_pairs={{0,8},{8,16},{16,24},{24,32},{32,40},{40,48},{48,56},{56,64},{64,7... | collective-permute-start | bytes 786440 | tf_op jit(solution)/shard_map/while/body/eval_jaxpr/ppermute | solution.py:15
  286.6 11.6 %collective-permute-start = (bf16[256,2,1,256]{3,0,2,1:T(8,128)(2,1)}, bf16[256,2,1,256]{3,0,2,1:T(8,128)(2,1)S(1)}, u32[]{:S(2)}, u32[]{:S(2)}) collective-permute-start(bf16[256,2,1,256]{3,0,2,1:T(8,128)(2,1)} %get-tuple-element.205), channel_id=1, source_target_pairs={{0,8},{8,16},{16,24},{24,32},{32,40},{40,48},{48,56},{56,64},{64,7... | collective-permute-start | bytes 786440 | tf_op jit(solution)/shard_map/while/body/eval_jaxpr/ppermute | solution.py:15
  298.9 14.6 %collective-permute-start = (bf16[256,2,1,256]{3,0,2,1:T(8,128)(2,1)}, bf16[256,2,1,256]{3,0,2,1:T(8,128)(2,1)S(1)}, u32[]{:S(2)}, u32[]{:S(2)}) collective-permute-start(bf16[256,2,1,256]{3,0,2,1:T(8,128)(2,1)} %get-tuple-element.205), channel_id=1, source_target_pairs={{0,8},{8,16},{16,24},{24,32},{32,40},{40,48},{48,56},{56,64},{64,7... | collective-permute-start | bytes 786440 | tf_op jit(solution)/shard_map/while/body/eval_jaxpr/ppermute | solution.py:15
  314.2 15.7 %collective-permute-start = (bf16[256,2,1,256]{3,0,2,1:T(8,128)(2,1)}, bf16[256,2,1,256]{3,0,2,1:T(8,128)(2,1)S(1)}, u32[]{:S(2)}, u32[]{:S(2)}) collective-permute-start(bf16[256,2,1,256]{3,0,2,1:T(8,128)(2,1)} %get-tuple-element.205), channel_id=1, source_target_pairs={{0,8},{8,16},{16,24},{24,32},{32,40},{40,48},{48,56},{56,64},{64,7... | collective-permute-start | bytes 786440 | tf_op jit(solution)/shard_map/while/body/eval_jaxpr/ppermute | solution.py:15
  330.6 12.5 %collective-permute-start = (bf16[256,2,1,256]{3,0,2,1:T(8,128)(2,1)}, bf16[256,2,1,256]{3,0,2,1:T(8,128)(2,1)S(1)}, u32[]{:S(2)}, u32[]{:S(2)}) collective-permute-start(bf16[256,2,1,256]{3,0,2,1:T(8,128)(2,1)} %get-tuple-element.205), channel_id=1, source_target_pairs={{0,8},{8,16},{16,24},{24,32},{32,40},{40,48},{48,56},{56,64},{64,7... | collective-permute-start | bytes 786440 | tf_op jit(solution)/shard_map/while/body/eval_jaxpr/ppermute | solution.py:15
  343.8 15.7 %collective-permute-start = (bf16[256,2,1,256]{3,0,2,1:T(8,128)(2,1)}, bf16[256,2,1,256]{3,0,2,1:T(8,128)(2,1)S(1)}, u32[]{:S(2)}, u32[]{:S(2)}) collective-permute-start(bf16[256,2,1,256]{3,0,2,1:T(8,128)(2,1)} %get-tuple-element.205), channel_id=1, source_target_pairs={{0,8},{8,16},{16,24},{24,32},{32,40},{40,48},{48,56},{56,64},{64,7... | collective-permute-start | bytes 786440 | tf_op jit(solution)/shard_map/while/body/eval_jaxpr/ppermute | solution.py:15
  360.3 15.7 %collective-permute-start = (bf16[256,2,1,256]{3,0,2,1:T(8,128)(2,1)}, bf16[256,2,1,256]{3,0,2,1:T(8,128)(2,1)S(1)}, u32[]{:S(2)}, u32[]{:S(2)}) collective-permute-start(bf16[256,2,1,256]{3,0,2,1:T(8,128)(2,1)} %get-tuple-element.205), channel_id=1, source_target_pairs={{0,8},{8,16},{16,24},{24,32},{32,40},{40,48},{48,56},{56,64},{64,7... | collective-permute-start | bytes 786440 | tf_op jit(solution)/shard_map/while/body/eval_jaxpr/ppermute | solution.py:15
  376.7 12.5 %collective-permute-start = (bf16[256,2,1,256]{3,0,2,1:T(8,128)(2,1)}, bf16[256,2,1,256]{3,0,2,1:T(8,128)(2,1)S(1)}, u32[]{:S(2)}, u32[]{:S(2)}) collective-permute-start(bf16[256,2,1,256]{3,0,2,1:T(8,128)(2,1)} %get-tuple-element.205), channel_id=1, source_target_pairs={{0,8},{8,16},{16,24},{24,32},{32,40},{40,48},{48,56},{56,64},{64,7... | collective-permute-start | bytes 786440 | tf_op jit(solution)/shard_map/while/body/eval_jaxpr/ppermute | solution.py:15
  390.0 15.7 %collective-permute-start = (bf16[256,2,1,256]{3,0,2,1:T(8,128)(2,1)}, bf16[256,2,1,256]{3,0,2,1:T(8,128)(2,1)S(1)}, u32[]{:S(2)}, u32[]{:S(2)}) collective-permute-start(bf16[256,2,1,256]{3,0,2,1:T(8,128)(2,1)} %get-tuple-element.205), channel_id=1, source_target_pairs={{0,8},{8,16},{16,24},{24,32},{32,40},{40,48},{48,56},{56,64},{64,7... | collective-permute-start | bytes 786440 | tf_op jit(solution)/shard_map/while/body/eval_jaxpr/ppermute | solution.py:15
  406.4 15.7 %collective-permute-start = (bf16[256,2,1,256]{3,0,2,1:T(8,128)(2,1)}, bf16[256,2,1,256]{3,0,2,1:T(8,128)(2,1)S(1)}, u32[]{:S(2)}, u32[]{:S(2)}) collective-permute-start(bf16[256,2,1,256]{3,0,2,1:T(8,128)(2,1)} %get-tuple-element.205), channel_id=1, source_target_pairs={{0,8},{8,16},{16,24},{24,32},{32,40},{40,48},{48,56},{56,64},{64,7... | collective-permute-start | bytes 786440 | tf_op jit(solution)/shard_map/while/body/eval_jaxpr/ppermute | solution.py:15
  409.0 10.7 %collective-permute-start.1 = (s32[256]{0:T(256)}, s32[256]{0:T(256)S(1)}, u32[]{:S(2)}, u32[]{:S(2)}) collective-permute-start(s32[256]{0:T(256)} %get-tuple-element.206), channel_id=1, source_target_pairs={{0,8},{8,16},{16,24},{24,32},{32,40},{40,48},{48,56},{56,64},{64,7... | collective-permute-start | bytes 3080 | tf_op jit(solution)/shard_map/while/body/eval_jaxpr/ppermute | solution.py:15
  422.9 12.5 %collective-permute-start = (bf16[256,2,1,256]{3,0,2,1:T(8,128)(2,1)}, bf16[256,2,1,256]{3,0,2,1:T(8,128)(2,1)S(1)}, u32[]{:S(2)}, u32[]{:S(2)}) collective-permute-start(bf16[256,2,1,256]{3,0,2,1:T(8,128)(2,1)} %get-tuple-element.205), channel_id=1, source_target_pairs={{0,8},{8,16},{16,24},{24,32},{32,40},{40,48},{48,56},{56,64},{64,7... | collective-permute-start | bytes 786440 | tf_op jit(solution)/shard_map/while/body/eval_jaxpr/ppermute | solution.py:15
  436.1 12.5 %collective-permute-start = (bf16[256,2,1,256]{3,0,2,1:T(8,128)(2,1)}, bf16[256,2,1,256]{3,0,2,1:T(8,128)(2,1)S(1)}, u32[]{:S(2)}, u32[]{:S(2)}) collective-permute-start(bf16[256,2,1,256]{3,0,2,1:T(8,128)(2,1)} %get-tuple-element.205), channel_id=1, source_target_pairs={{0,8},{8,16},{16,24},{24,32},{32,40},{40,48},{48,56},{56,64},{64,7... | collective-permute-start | bytes 786440 | tf_op jit(solution)/shard_map/while/body/eval_jaxpr/ppermute | solution.py:15
  449.3 12.5 %collective-permute-start = (bf16[256,2,1,256]{3,0,2,1:T(8,128)(2,1)}, bf16[256,2,1,256]{3,0,2,1:T(8,128)(2,1)S(1)}, u32[]{:S(2)}, u32[]{:S(2)}) collective-permute-start(bf16[256,2,1,256]{3,0,2,1:T(8,128)(2,1)} %get-tuple-element.205), channel_id=1, source_target_pairs={{0,8},{8,16},{16,24},{24,32},{32,40},{40,48},{48,56},{56,64},{64,7... | collective-permute-start | bytes 786440 | tf_op jit(solution)/shard_map/while/body/eval_jaxpr/ppermute | solution.py:15
  462.5 12.5 %collective-permute-start = (bf16[256,2,1,256]{3,0,2,1:T(8,128)(2,1)}, bf16[256,2,1,256]{3,0,2,1:T(8,128)(2,1)S(1)}, u32[]{:S(2)}, u32[]{:S(2)}) collective-permute-start(bf16[256,2,1,256]{3,0,2,1:T(8,128)(2,1)} %get-tuple-element.205), channel_id=1, source_target_pairs={{0,8},{8,16},{16,24},{24,32},{32,40},{40,48},{48,56},{56,64},{64,7... | collective-permute-start | bytes 786440 | tf_op jit(solution)/shard_map/while/body/eval_jaxpr/ppermute | solution.py:15
  475.8 12.5 %collective-permute-start = (bf16[256,2,1,256]{3,0,2,1:T(8,128)(2,1)}, bf16[256,2,1,256]{3,0,2,1:T(8,128)(2,1)S(1)}, u32[]{:S(2)}, u32[]{:S(2)}) collective-permute-start(bf16[256,2,1,256]{3,0,2,1:T(8,128)(2,1)} %get-tuple-element.205), channel_id=1, source_target_pairs={{0,8},{8,16},{16,24},{24,32},{32,40},{40,48},{48,56},{56,64},{64,7... | collective-permute-start | bytes 786440 | tf_op jit(solution)/shard_map/while/body/eval_jaxpr/ppermute | solution.py:15
  489.0 12.5 %collective-permute-start = (bf16[256,2,1,256]{3,0,2,1:T(8,128)(2,1)}, bf16[256,2,1,256]{3,0,2,1:T(8,128)(2,1)S(1)}, u32[]{:S(2)}, u32[]{:S(2)}) collective-permute-start(bf16[256,2,1,256]{3,0,2,1:T(8,128)(2,1)} %get-tuple-element.205), channel_id=1, source_target_pairs={{0,8},{8,16},{16,24},{24,32},{32,40},{40,48},{48,56},{56,64},{64,7... | collective-permute-start | bytes 786440 | tf_op jit(solution)/shard_map/while/body/eval_jaxpr/ppermute | solution.py:15
  502.2 12.5 %collective-permute-start = (bf16[256,2,1,256]{3,0,2,1:T(8,128)(2,1)}, bf16[256,2,1,256]{3,0,2,1:T(8,128)(2,1)S(1)}, u32[]{:S(2)}, u32[]{:S(2)}) collective-permute-start(bf16[256,2,1,256]{3,0,2,1:T(8,128)(2,1)} %get-tuple-element.205), channel_id=1, source_target_pairs={{0,8},{8,16},{16,24},{24,32},{32,40},{40,48},{48,56},{56,64},{64,7... | collective-permute-start | bytes 786440 | tf_op jit(solution)/shard_map/while/body/eval_jaxpr/ppermute | solution.py:15
  515.4 12.5 %collective-permute-start = (bf16[256,2,1,256]{3,0,2,1:T(8,128)(2,1)}, bf16[256,2,1,256]{3,0,2,1:T(8,128)(2,1)S(1)}, u32[]{:S(2)}, u32[]{:S(2)}) collective-permute-start(bf16[256,2,1,256]{3,0,2,1:T(8,128)(2,1)} %get-tuple-element.205), channel_id=1, source_target_pairs={{0,8},{8,16},{16,24},{24,32},{32,40},{40,48},{48,56},{56,64},{64,7... | collective-permute-start | bytes 786440 | tf_op jit(solution)/shard_map/while/body/eval_jaxpr/ppermute | solution.py:15
  528.7 12.5 %collective-permute-start = (bf16[256,2,1,256]{3,0,2,1:T(8,128)(2,1)}, bf16[256,2,1,256]{3,0,2,1:T(8,128)(2,1)S(1)}, u32[]{:S(2)}, u32[]{:S(2)}) collective-permute-start(bf16[256,2,1,256]{3,0,2,1:T(8,128)(2,1)} %get-tuple-element.205), channel_id=1, source_target_pairs={{0,8},{8,16},{16,24},{24,32},{32,40},{40,48},{48,56},{56,64},{64,7... | collective-permute-start | bytes 786440 | tf_op jit(solution)/shard_map/while/body/eval_jaxpr/ppermute | solution.py:15
  (48 other events, 535.1 us)
Sparse Core Ops, SparseCore 0:
  11.1 72.0 all-gather.1
  544.8 163.9 reduce-scatter.1
where the time goes:
time: 720 us; the launch traced here: 716 us
  starting transfers between devices  307 us (43%)
  waiting for transfers between devices  239 us (33%)
  local copies, waits for them, and re-layouts  89.6 us (12%)
  loops' own time  40.4 us (6%)
  matrix products  15 us (2%)
  between operations  14.2 us (2%)
  other arithmetic  10.1 us (1%)
    ppermute x66, starting transfers between devices, passed_along(): lax.ppermute(value, axis, [(source, source + steps) for source in range(f...  307 us
    reduce_scatter x1, waiting for transfers between devices, per_device(): lax.psum_scatter(partial_value.astype(jnp.bfloat16), 'tp', scatter_dimens...  143 us
    all_gather x1, waiting for transfers between devices, per_device(): whole_rows = lax.all_gather(hidden_in, 'tp', axis=1, tiled=True)  70.7 us
    while x64, local copies, waits for them, and re-layouts  41 us
    another operation x1, loops' own time, per_device(): lax.fori_loop(0, reach, relay_step, (pair_block, own_marks, carry_state))[2]  40.4 us
    ppermute x66, waiting for transfers between devices, passed_along(): lax.ppermute(value, axis, [(source, source + steps) for source in range(f...  24.8 us
    slice x32, local copies, waits for them, and re-layouts, visit_block(): tail_mark = key_marks[key_marks.shape[0] - 1]  20.7 us
    slice x32, local copies, waits for them, and re-layouts, visit_block(): relevant = tail_mark == query_marks[0]  16.2 us
  transfers between devices with their start and end apart: 68, of which 36 were waited for; matrix products, arithmetic and copies ran while one was open for 10% of the time, Pallas kernels for 0%

commit v1 on v0

--- a/solution.py
+++ b/solution.py
@@ -82,7 +82,9 @@
     local_heads = w_out.shape[0] // HD
     my_index = lax.axis_index("ctx")
     reach = lax.axis_size("ctx") // 2
-    whole_rows = lax.all_gather(hidden_in, "tp", axis=1, tiled=True)
+    whole_rows = jnp.concatenate(
+        lax.all_to_all(jnp.stack([hidden_in] * lax.axis_size("tp")), "tp", 0, 0), axis=1
+    )
     normed = normalize(whole_rows.astype(jnp.float32), ln_gain, ln_bias).astype(jnp.bfloat16)
     projected = jnp.einsum("td,jdh->tjh", normed, w_qkv, preferred_element_type=jnp.float32)
     starts = jnp.cumsum(prompt_lengths) - prompt_lengths

time: 720 us -> 696 us (0.967)
  waiting for transfers between devices: 239 us -> 191 us
  starting transfers between devices: 307 us -> 325 us
    all_gather x1 -> x0, waiting for transfers between devices: 70.7 us -> none  [per_device(): whole_rows = lax.all_gather(hidden_in, 'tp', axis=1, tiled=True)]
    all_to_all x0 -> x1, waiting for transfers between devices: none -> 27.3 us  [per_device(): lax.all_to_all(jnp.stack([hidden_in] * lax.axis_size('tp')), 'tp', 0, 0)]
    all_to_all x0 -> x1, starting transfers between devices: none -> 12.7 us  [per_device(): lax.all_to_all(jnp.stack([hidden_in] * lax.axis_size('tp')), 'tp', 0, 0)]
where the time goes in v1:
time: 696 us; the launch traced here: 692 us
  starting transfers between devices  325 us (47%)
  waiting for transfers between devices  191 us (27%)
  local copies, waits for them, and re-layouts  94.8 us (14%)
  loops' own time  43.2 us (6%)
  matrix products  14.8 us (2%)
  between operations  14.2 us (2%)
  other arithmetic  9.35 us (1%)
    ppermute x66, starting transfers between devices, passed_along(): lax.ppermute(value, axis, [(source, source + steps) for source in range(f...  312 us
    reduce_scatter x1, waiting for transfers between devices, per_device(): lax.psum_scatter(partial_value.astype(jnp.bfloat16), 'tp', scatter_dimens...  145 us
    another operation x1, loops' own time, per_device(): lax.fori_loop(0, reach, relay_step, (pair_block, own_marks, carry_state))[2]  43.1 us
    while x64, local copies, waits for them, and re-layouts  40.9 us
    all_to_all x1, waiting for transfers between devices, per_device(): lax.all_to_all(jnp.stack([hidden_in] * lax.axis_size('tp')), 'tp', 0, 0)  27.3 us
    slice x32, local copies, waits for them, and re-layouts, visit_block(): tail_mark = key_marks[key_marks.shape[0] - 1]  18.6 us
    slice x32, local copies, waits for them, and re-layouts, visit_block(): relevant = tail_mark == query_marks[0]  18.5 us
    ppermute x66, waiting for transfers between devices, passed_along(): lax.ppermute(value, axis, [(source, source + steps) for source in range(f...  18.5 us
  transfers between devices with their start and end apart: 68, of which 36 were waited for; matrix products, arithmetic and copies ran while one was open for 10% of the time, Pallas kernels for 0%

profile of v1, /device:TPU:8, one launch (start us, length us, event | category | flops | bytes accessed | tf_op | source)
XLA Modules:
  0.0 691.6 jit_solution(15824494934861926205)
XLA Ops:
  9.4 12.7 %all-to-all-start = ((bf16[8,256,256]{2,1,0:T(8,128)(2,1)}), bf16[8,256,256]{2,1,0:T(8,128)(2,1)}, u32[]{:S(2)}, u32[]{:S(2)}) async-start(bf16[8,256,256]{2,1,0:T(8,128)(2,1)} %stack.6), calls=%async_computation | async-start | bytes 2097152 | tf_op jit(solution)/shard_map/all_to_all | solution.py:86
  23.7 27.3 %all-to-all-done = bf16[8,256,256]{2,1,0:T(8,128)(2,1)} async-done(((bf16[8,256,256]{2,1,0:T(8,128)(2,1)}), bf16[8,256,256]{2,1,0:T(8,128)(2,1)}, u32[]{:S(2)}, u32[]{:S(2)}) %all-to-all-start) | async-done | bytes 1048608 | tf_op jit(solution)/shard_map/all_to_all | solution.py:86
  68.0 447.9 %while.18 = (s32[]{:T(128)}, bf16[256,2,1,256]{3,0,2,1:T(8,128)(2,1)}, s32[256]{0:T(256)}, f32[1,256]{1,0:T(1,128)S(1)}, f32[1,256]{1,0:T(1,128)S(1)}, /*index=5...) while((s32[]{:T(128)}, bf16[256,2,1,256]{3,0,2,1:T(8,128)(2,1)}, ...), condition=%wide.region_11.12_spmd, body=%wide.region_6.11_spmd.sunk | while | flops 67764736 | bytes 3431739 | solution.py:115
  123.4 8.0 %collective-permute-start.1 = (s32[256]{0:T(256)}, s32[256]{0:T(256)S(1)}, u32[]{:S(2)}, u32[]{:S(2)}) collective-permute-start(s32[256]{0:T(256)} %get-tuple-element.222), channel_id=1, source_target_pairs={{0,8},{8,16},{16,24},{24,32},{32,40},{40,48},{48,56},{56,64},{64,7... | collective-permute-start | bytes 3080 | tf_op jit(solution)/shard_map/while/body/eval_jaxpr/ppermute | solution.py:15
  138.3 5.4 collective-permute-start.1
  147.8 6.1 collective-permute-start
  166.2 8.6 %collective-permute-start.1 = (s32[256]{0:T(256)}, s32[256]{0:T(256)S(1)}, u32[]{:S(2)}, u32[]{:S(2)}) collective-permute-start(s32[256]{0:T(256)} %get-tuple-element.222), channel_id=1, source_target_pairs={{0,8},{8,16},{16,24},{24,32},{32,40},{40,48},{48,56},{56,64},{64,7... | collective-permute-start | bytes 3080 | tf_op jit(solution)/shard_map/while/body/eval_jaxpr/ppermute | solution.py:15
  181.8 5.4 collective-permute-start.1
  191.3 6.1 collective-permute-start
  209.7 8.6 %collective-permute-start.1 = (s32[256]{0:T(256)}, s32[256]{0:T(256)S(1)}, u32[]{:S(2)}, u32[]{:S(2)}) collective-permute-start(s32[256]{0:T(256)} %get-tuple-element.222), channel_id=1, source_target_pairs={{0,8},{8,16},{16,24},{24,32},{32,40},{40,48},{48,56},{56,64},{64,7... | collective-permute-start | bytes 3080 | tf_op jit(solution)/shard_map/while/body/eval_jaxpr/ppermute | solution.py:15
  237.6 5.4 collective-permute-start.1
  271.8 5.9 collective-permute-start
  277.7 6.1 collective-permute-start.1
  290.9 9.3 %collective-permute-start.1 = (s32[256]{0:T(256)}, s32[256]{0:T(256)S(1)}, u32[]{:S(2)}, u32[]{:S(2)}) collective-permute-start(s32[256]{0:T(256)} %get-tuple-element.222), channel_id=1, source_target_pairs={{0,8},{8,16},{16,24},{24,32},{32,40},{40,48},{48,56},{56,64},{64,7... | collective-permute-start | bytes 3080 | tf_op jit(solution)/shard_map/while/body/eval_jaxpr/ppermute | solution.py:15
  307.4 6.1 collective-permute-start.1
  317.5 6.3 collective-permute-start
  323.9 6.1 collective-permute-start.1
  337.1 9.3 %collective-permute-start.1 = (s32[256]{0:T(256)}, s32[256]{0:T(256)S(1)}, u32[]{:S(2)}, u32[]{:S(2)}) collective-permute-start(s32[256]{0:T(256)} %get-tuple-element.222), channel_id=1, source_target_pairs={{0,8},{8,16},{16,24},{24,32},{32,40},{40,48},{48,56},{56,64},{64,7... | collective-permute-start | bytes 3080 | tf_op jit(solution)/shard_map/while/body/eval_jaxpr/ppermute | solution.py:15
  353.6 6.1 collective-permute-start.1
  363.7 6.3 collective-permute-start
  370.0 6.1 collective-permute-start.1
  383.3 9.3 %collective-permute-start.1 = (s32[256]{0:T(256)}, s32[256]{0:T(256)S(1)}, u32[]{:S(2)}, u32[]{:S(2)}) collective-permute-start(s32[256]{0:T(256)} %get-tuple-element.222), channel_id=1, source_target_pairs={{0,8},{8,16},{16,24},{24,32},{32,40},{40,48},{48,56},{56,64},{64,7... | collective-permute-start | bytes 3080 | tf_op jit(solution)/shard_map/while/body/eval_jaxpr/ppermute | solution.py:15
  399.7 6.1 collective-permute-start.1
  413.0 6.1 collective-permute-start.1
  426.2 6.1 collective-permute-start.1
  439.5 6.1 collective-permute-start.1
  452.7 6.1 collective-permute-start.1
  466.0 6.1 collective-permute-start.1
  479.2 6.1 collective-permute-start.1
  492.5 6.1 collective-permute-start.1
  505.7 6.1 collective-permute-start.1
  539.8 144.9 %reduce-scatter.2.cloned.1.call-done = bf16[256,256]{1,0:T(8,128)(2,1)} async-done(((bf16[256,2048]{1,0:T(8,128)(2,1)}), bf16[256,256]{1,0:T(8,128)(2,1)}) %reduce-scatter.2.cloned.1.call-update) | async-done | bytes 131088 | tf_op jit(solution)/shard_map/reduce_scatter | solution.py:124
  (349 shorter events, 270.2 us)
Async XLA Ops:
  9.4 41.6 %all-to-all-start = ((bf16[8,256,256]{2,1,0:T(8,128)(2,1)}), bf16[8,256,256]{2,1,0:T(8,128)(2,1)}, u32[]{:S(2)}, u32[]{:S(2)}) async-start(bf16[8,256,256]{2,1,0:T(8,128)(2,1)} %stack.6), calls=%async_computation | async-start | bytes 2097152 | tf_op jit(solution)/shard_map/all_to_all | solution.py:86
  22.1 662.6 %reduce-scatter.2.cloned.1.call-start = ((), (), s32[]{:S(2)}) async-start(), calls=%async_computation.2 | async-start | bytes 1179648 | tf_op jit(solution)/shard_map/reduce_scatter | solution.py:124
  68.0 10.4 %collective-permute-start = (bf16[256,2,1,256]{3,0,2,1:T(8,128)(2,1)}, bf16[256,2,1,256]{3,0,2,1:T(8,128)(2,1)S(1)}, u32[]{:S(2)}, u32[]{:S(2)}) collective-permute-start(bf16[256,2,1,256]{3,0,2,1:T(8,128)(2,1)} %get-tuple-element.221), channel_id=1, source_target_pairs={{0,8},{8,16},{16,24},{24,32},{32,40},{40,48},{48,56},{56,64},{64,7... | collective-permute-start | bytes 786440 | tf_op jit(solution)/shard_map/while/body/eval_jaxpr/ppermute | solution.py:15
  107.8 12.1 %collective-permute-start = (bf16[256,2,1,256]{3,0,2,1:T(8,128)(2,1)}, bf16[256,2,1,256]{3,0,2,1:T(8,128)(2,1)S(1)}, u32[]{:S(2)}, u32[]{:S(2)}) collective-permute-start(bf16[256,2,1,256]{3,0,2,1:T(8,128)(2,1)} %get-tuple-element.221), channel_id=1, source_target_pairs={{0,8},{8,16},{16,24},{24,32},{32,40},{40,48},{48,56},{56,64},{64,7... | collective-permute-start | bytes 786440 | tf_op jit(solution)/shard_map/while/body/eval_jaxpr/ppermute | solution.py:15
  120.6 14.1 %collective-permute-start = (bf16[256,2,1,256]{3,0,2,1:T(8,128)(2,1)}, bf16[256,2,1,256]{3,0,2,1:T(8,128)(2,1)S(1)}, u32[]{:S(2)}, u32[]{:S(2)}) collective-permute-start(bf16[256,2,1,256]{3,0,2,1:T(8,128)(2,1)} %get-tuple-element.221), channel_id=1, source_target_pairs={{0,8},{8,16},{16,24},{24,32},{32,40},{40,48},{48,56},{56,64},{64,7... | collective-permute-start | bytes 786440 | tf_op jit(solution)/shard_map/while/body/eval_jaxpr/ppermute | solution.py:15
  135.4 11.6 %collective-permute-start = (bf16[256,2,1,256]{3,0,2,1:T(8,128)(2,1)}, bf16[256,2,1,256]{3,0,2,1:T(8,128)(2,1)S(1)}, u32[]{:S(2)}, u32[]{:S(2)}) collective-permute-start(bf16[256,2,1,256]{3,0,2,1:T(8,128)(2,1)} %get-tuple-element.221), channel_id=1, source_target_pairs={{0,8},{8,16},{16,24},{24,32},{32,40},{40,48},{48,56},{56,64},{64,7... | collective-permute-start | bytes 786440 | tf_op jit(solution)/shard_map/while/body/eval_jaxpr/ppermute | solution.py:15
  147.8 14.9 %collective-permute-start = (bf16[256,2,1,256]{3,0,2,1:T(8,128)(2,1)}, bf16[256,2,1,256]{3,0,2,1:T(8,128)(2,1)S(1)}, u32[]{:S(2)}, u32[]{:S(2)}) collective-permute-start(bf16[256,2,1,256]{3,0,2,1:T(8,128)(2,1)} %get-tuple-element.221), channel_id=1, source_target_pairs={{0,8},{8,16},{16,24},{24,32},{32,40},{40,48},{48,56},{56,64},{64,7... | collective-permute-start | bytes 786440 | tf_op jit(solution)/shard_map/while/body/eval_jaxpr/ppermute | solution.py:15
  163.4 14.9 %collective-permute-start = (bf16[256,2,1,256]{3,0,2,1:T(8,128)(2,1)}, bf16[256,2,1,256]{3,0,2,1:T(8,128)(2,1)S(1)}, u32[]{:S(2)}, u32[]{:S(2)}) collective-permute-start(bf16[256,2,1,256]{3,0,2,1:T(8,128)(2,1)} %get-tuple-element.221), channel_id=1, source_target_pairs={{0,8},{8,16},{16,24},{24,32},{32,40},{40,48},{48,56},{56,64},{64,7... | collective-permute-start | bytes 786440 | tf_op jit(solution)/shard_map/while/body/eval_jaxpr/ppermute | solution.py:15
  178.9 11.6 %collective-permute-start = (bf16[256,2,1,256]{3,0,2,1:T(8,128)(2,1)}, bf16[256,2,1,256]{3,0,2,1:T(8,128)(2,1)S(1)}, u32[]{:S(2)}, u32[]{:S(2)}) collective-permute-start(bf16[256,2,1,256]{3,0,2,1:T(8,128)(2,1)} %get-tuple-element.221), channel_id=1, source_target_pairs={{0,8},{8,16},{16,24},{24,32},{32,40},{40,48},{48,56},{56,64},{64,7... | collective-permute-start | bytes 786440 | tf_op jit(solution)/shard_map/while/body/eval_jaxpr/ppermute | solution.py:15
  191.3 14.9 %collective-permute-start = (bf16[256,2,1,256]{3,0,2,1:T(8,128)(2,1)}, bf16[256,2,1,256]{3,0,2,1:T(8,128)(2,1)S(1)}, u32[]{:S(2)}, u32[]{:S(2)}) collective-permute-start(bf16[256,2,1,256]{3,0,2,1:T(8,128)(2,1)} %get-tuple-element.221), channel_id=1, source_target_pairs={{0,8},{8,16},{16,24},{24,32},{32,40},{40,48},{48,56},{56,64},{64,7... | collective-permute-start | bytes 786440 | tf_op jit(solution)/shard_map/while/body/eval_jaxpr/ppermute | solution.py:15
  206.8 14.9 %collective-permute-start = (bf16[256,2,1,256]{3,0,2,1:T(8,128)(2,1)}, bf16[256,2,1,256]{3,0,2,1:T(8,128)(2,1)S(1)}, u32[]{:S(2)}, u32[]{:S(2)}) collective-permute-start(bf16[256,2,1,256]{3,0,2,1:T(8,128)(2,1)} %get-tuple-element.221), channel_id=1, source_target_pairs={{0,8},{8,16},{16,24},{24,32},{32,40},{40,48},{48,56},{56,64},{64,7... | collective-permute-start | bytes 786440 | tf_op jit(solution)/shard_map/while/body/eval_jaxpr/ppermute | solution.py:15
  222.4 11.6 %collective-permute-start = (bf16[256,2,1,256]{3,0,2,1:T(8,128)(2,1)}, bf16[256,2,1,256]{3,0,2,1:T(8,128)(2,1)S(1)}, u32[]{:S(2)}, u32[]{:S(2)}) collective-permute-start(bf16[256,2,1,256]{3,0,2,1:T(8,128)(2,1)} %get-tuple-element.221), channel_id=1, source_target_pairs={{0,8},{8,16},{16,24},{24,32},{32,40},{40,48},{48,56},{56,64},{64,7... | collective-permute-start | bytes 786440 | tf_op jit(solution)/shard_map/while/body/eval_jaxpr/ppermute | solution.py:15
  234.8 11.6 %collective-permute-start = (bf16[256,2,1,256]{3,0,2,1:T(8,128)(2,1)}, bf16[256,2,1,256]{3,0,2,1:T(8,128)(2,1)S(1)}, u32[]{:S(2)}, u32[]{:S(2)}) collective-permute-start(bf16[256,2,1,256]{3,0,2,1:T(8,128)(2,1)} %get-tuple-element.221), channel_id=1, source_target_pairs={{0,8},{8,16},{16,24},{24,32},{32,40},{40,48},{48,56},{56,64},{64,7... | collective-permute-start | bytes 786440 | tf_op jit(solution)/shard_map/while/body/eval_jaxpr/ppermute | solution.py:15
  247.1 11.6 %collective-permute-start = (bf16[256,2,1,256]{3,0,2,1:T(8,128)(2,1)}, bf16[256,2,1,256]{3,0,2,1:T(8,128)(2,1)S(1)}, u32[]{:S(2)}, u32[]{:S(2)}) collective-permute-start(bf16[256,2,1,256]{3,0,2,1:T(8,128)(2,1)} %get-tuple-element.221), channel_id=1, source_target_pairs={{0,8},{8,16},{16,24},{24,32},{32,40},{40,48},{48,56},{56,64},{64,7... | collective-permute-start | bytes 786440 | tf_op jit(solution)/shard_map/while/body/eval_jaxpr/ppermute | solution.py:15
  259.5 11.6 %collective-permute-start = (bf16[256,2,1,256]{3,0,2,1:T(8,128)(2,1)}, bf16[256,2,1,256]{3,0,2,1:T(8,128)(2,1)S(1)}, u32[]{:S(2)}, u32[]{:S(2)}) collective-permute-start(bf16[256,2,1,256]{3,0,2,1:T(8,128)(2,1)} %get-tuple-element.221), channel_id=1, source_target_pairs={{0,8},{8,16},{16,24},{24,32},{32,40},{40,48},{48,56},{56,64},{64,7... | collective-permute-start | bytes 786440 | tf_op jit(solution)/shard_map/while/body/eval_jaxpr/ppermute | solution.py:15
  271.8 15.3 %collective-permute-start = (bf16[256,2,1,256]{3,0,2,1:T(8,128)(2,1)}, bf16[256,2,1,256]{3,0,2,1:T(8,128)(2,1)S(1)}, u32[]{:S(2)}, u32[]{:S(2)}) collective-permute-start(bf16[256,2,1,256]{3,0,2,1:T(8,128)(2,1)} %get-tuple-element.221), channel_id=1, source_target_pairs={{0,8},{8,16},{16,24},{24,32},{32,40},{40,48},{48,56},{56,64},{64,7... | collective-permute-start | bytes 786440 | tf_op jit(solution)/shard_map/while/body/eval_jaxpr/ppermute | solution.py:15
  287.8 15.8 %collective-permute-start = (bf16[256,2,1,256]{3,0,2,1:T(8,128)(2,1)}, bf16[256,2,1,256]{3,0,2,1:T(8,128)(2,1)S(1)}, u32[]{:S(2)}, u32[]{:S(2)}) collective-permute-start(bf16[256,2,1,256]{3,0,2,1:T(8,128)(2,1)} %get-tuple-element.221), channel_id=1, source_target_pairs={{0,8},{8,16},{16,24},{24,32},{32,40},{40,48},{48,56},{56,64},{64,7... | collective-permute-start | bytes 786440 | tf_op jit(solution)/shard_map/while/body/eval_jaxpr/ppermute | solution.py:15
  304.3 12.5 %collective-permute-start = (bf16[256,2,1,256]{3,0,2,1:T(8,128)(2,1)}, bf16[256,2,1,256]{3,0,2,1:T(8,128)(2,1)S(1)}, u32[]{:S(2)}, u32[]{:S(2)}) collective-permute-start(bf16[256,2,1,256]{3,0,2,1:T(8,128)(2,1)} %get-tuple-element.221), channel_id=1, source_target_pairs={{0,8},{8,16},{16,24},{24,32},{32,40},{40,48},{48,56},{56,64},{64,7... | collective-permute-start | bytes 786440 | tf_op jit(solution)/shard_map/while/body/eval_jaxpr/ppermute | solution.py:15
  317.5 15.8 %collective-permute-start = (bf16[256,2,1,256]{3,0,2,1:T(8,128)(2,1)}, bf16[256,2,1,256]{3,0,2,1:T(8,128)(2,1)S(1)}, u32[]{:S(2)}, u32[]{:S(2)}) collective-permute-start(bf16[256,2,1,256]{3,0,2,1:T(8,128)(2,1)} %get-tuple-element.221), channel_id=1, source_target_pairs={{0,8},{8,16},{16,24},{24,32},{32,40},{40,48},{48,56},{56,64},{64,7... | collective-permute-start | bytes 786440 | tf_op jit(solution)/shard_map/while/body/eval_jaxpr/ppermute | solution.py:15
  334.0 15.8 %collective-permute-start = (bf16[256,2,1,256]{3,0,2,1:T(8,128)(2,1)}, bf16[256,2,1,256]{3,0,2,1:T(8,128)(2,1)S(1)}, u32[]{:S(2)}, u32[]{:S(2)}) collective-permute-start(bf16[256,2,1,256]{3,0,2,1:T(8,128)(2,1)} %get-tuple-element.221), channel_id=1, source_target_pairs={{0,8},{8,16},{16,24},{24,32},{32,40},{40,48},{48,56},{56,64},{64,7... | collective-permute-start | bytes 786440 | tf_op jit(solution)/shard_map/while/body/eval_jaxpr/ppermute | solution.py:15
  350.5 12.5 %collective-permute-start = (bf16[256,2,1,256]{3,0,2,1:T(8,128)(2,1)}, bf16[256,2,1,256]{3,0,2,1:T(8,128)(2,1)S(1)}, u32[]{:S(2)}, u32[]{:S(2)}) collective-permute-start(bf16[256,2,1,256]{3,0,2,1:T(8,128)(2,1)} %get-tuple-element.221), channel_id=1, source_target_pairs={{0,8},{8,16},{16,24},{24,32},{32,40},{40,48},{48,56},{56,64},{64,7... | collective-permute-start | bytes 786440 | tf_op jit(solution)/shard_map/while/body/eval_jaxpr/ppermute | solution.py:15
  363.7 15.8 %collective-permute-start = (bf16[256,2,1,256]{3,0,2,1:T(8,128)(2,1)}, bf16[256,2,1,256]{3,0,2,1:T(8,128)(2,1)S(1)}, u32[]{:S(2)}, u32[]{:S(2)}) collective-permute-start(bf16[256,2,1,256]{3,0,2,1:T(8,128)(2,1)} %get-tuple-element.221), channel_id=1, source_target_pairs={{0,8},{8,16},{16,24},{24,32},{32,40},{40,48},{48,56},{56,64},{64,7... | collective-permute-start | bytes 786440 | tf_op jit(solution)/shard_map/while/body/eval_jaxpr/ppermute | solution.py:15
  380.2 15.8 %collective-permute-start = (bf16[256,2,1,256]{3,0,2,1:T(8,128)(2,1)}, bf16[256,2,1,256]{3,0,2,1:T(8,128)(2,1)S(1)}, u32[]{:S(2)}, u32[]{:S(2)}) collective-permute-start(bf16[256,2,1,256]{3,0,2,1:T(8,128)(2,1)} %get-tuple-element.221), channel_id=1, source_target_pairs={{0,8},{8,16},{16,24},{24,32},{32,40},{40,48},{48,56},{56,64},{64,7... | collective-permute-start | bytes 786440 | tf_op jit(solution)/shard_map/while/body/eval_jaxpr/ppermute | solution.py:15
  396.6 12.5 %collective-permute-start = (bf16[256,2,1,256]{3,0,2,1:T(8,128)(2,1)}, bf16[256,2,1,256]{3,0,2,1:T(8,128)(2,1)S(1)}, u32[]{:S(2)}, u32[]{:S(2)}) collective-permute-start(bf16[256,2,1,256]{3,0,2,1:T(8,128)(2,1)} %get-tuple-element.221), channel_id=1, source_target_pairs={{0,8},{8,16},{16,24},{24,32},{32,40},{40,48},{48,56},{56,64},{64,7... | collective-permute-start | bytes 786440 | tf_op jit(solution)/shard_map/while/body/eval_jaxpr/ppermute | solution.py:15
  409.9 12.5 %collective-permute-start = (bf16[256,2,1,256]{3,0,2,1:T(8,128)(2,1)}, bf16[256,2,1,256]{3,0,2,1:T(8,128)(2,1)S(1)}, u32[]{:S(2)}, u32[]{:S(2)}) collective-permute-start(bf16[256,2,1,256]{3,0,2,1:T(8,128)(2,1)} %get-tuple-element.221), channel_id=1, source_target_pairs={{0,8},{8,16},{16,24},{24,32},{32,40},{40,48},{48,56},{56,64},{64,7... | collective-permute-start | bytes 786440 | tf_op jit(solution)/shard_map/while/body/eval_jaxpr/ppermute | solution.py:15
  423.1 12.5 %collective-permute-start = (bf16[256,2,1,256]{3,0,2,1:T(8,128)(2,1)}, bf16[256,2,1,256]{3,0,2,1:T(8,128)(2,1)S(1)}, u32[]{:S(2)}, u32[]{:S(2)}) collective-permute-start(bf16[256,2,1,256]{3,0,2,1:T(8,128)(2,1)} %get-tuple-element.221), channel_id=1, source_target_pairs={{0,8},{8,16},{16,24},{24,32},{32,40},{40,48},{48,56},{56,64},{64,7... | collective-permute-start | bytes 786440 | tf_op jit(solution)/shard_map/while/body/eval_jaxpr/ppermute | solution.py:15
  436.4 12.5 %collective-permute-start = (bf16[256,2,1,256]{3,0,2,1:T(8,128)(2,1)}, bf16[256,2,1,256]{3,0,2,1:T(8,128)(2,1)S(1)}, u32[]{:S(2)}, u32[]{:S(2)}) collective-permute-start(bf16[256,2,1,256]{3,0,2,1:T(8,128)(2,1)} %get-tuple-element.221), channel_id=1, source_target_pairs={{0,8},{8,16},{16,24},{24,32},{32,40},{40,48},{48,56},{56,64},{64,7... | collective-permute-start | bytes 786440 | tf_op jit(solution)/shard_map/while/body/eval_jaxpr/ppermute | solution.py:15
  449.6 12.5 %collective-permute-start = (bf16[256,2,1,256]{3,0,2,1:T(8,128)(2,1)}, bf16[256,2,1,256]{3,0,2,1:T(8,128)(2,1)S(1)}, u32[]{:S(2)}, u32[]{:S(2)}) collective-permute-start(bf16[256,2,1,256]{3,0,2,1:T(8,128)(2,1)} %get-tuple-element.221), channel_id=1, source_target_pairs={{0,8},{8,16},{16,24},{24,32},{32,40},{40,48},{48,56},{56,64},{64,7... | collective-permute-start | bytes 786440 | tf_op jit(solution)/shard_map/while/body/eval_jaxpr/ppermute | solution.py:15
  462.9 12.5 %collective-permute-start = (bf16[256,2,1,256]{3,0,2,1:T(8,128)(2,1)}, bf16[256,2,1,256]{3,0,2,1:T(8,128)(2,1)S(1)}, u32[]{:S(2)}, u32[]{:S(2)}) collective-permute-start(bf16[256,2,1,256]{3,0,2,1:T(8,128)(2,1)} %get-tuple-element.221), channel_id=1, source_target_pairs={{0,8},{8,16},{16,24},{24,32},{32,40},{40,48},{48,56},{56,64},{64,7... | collective-permute-start | bytes 786440 | tf_op jit(solution)/shard_map/while/body/eval_jaxpr/ppermute | solution.py:15
  476.1 12.5 %collective-permute-start = (bf16[256,2,1,256]{3,0,2,1:T(8,128)(2,1)}, bf16[256,2,1,256]{3,0,2,1:T(8,128)(2,1)S(1)}, u32[]{:S(2)}, u32[]{:S(2)}) collective-permute-start(bf16[256,2,1,256]{3,0,2,1:T(8,128)(2,1)} %get-tuple-element.221), channel_id=1, source_target_pairs={{0,8},{8,16},{16,24},{24,32},{32,40},{40,48},{48,56},{56,64},{64,7... | collective-permute-start | bytes 786440 | tf_op jit(solution)/shard_map/while/body/eval_jaxpr/ppermute | solution.py:15
  489.4 12.5 %collective-permute-start = (bf16[256,2,1,256]{3,0,2,1:T(8,128)(2,1)}, bf16[256,2,1,256]{3,0,2,1:T(8,128)(2,1)S(1)}, u32[]{:S(2)}, u32[]{:S(2)}) collective-permute-start(bf16[256,2,1,256]{3,0,2,1:T(8,128)(2,1)} %get-tuple-element.221), channel_id=1, source_target_pairs={{0,8},{8,16},{16,24},{24,32},{32,40},{40,48},{48,56},{56,64},{64,7... | collective-permute-start | bytes 786440 | tf_op jit(solution)/shard_map/while/body/eval_jaxpr/ppermute | solution.py:15
  502.6 12.5 %collective-permute-start = (bf16[256,2,1,256]{3,0,2,1:T(8,128)(2,1)}, bf16[256,2,1,256]{3,0,2,1:T(8,128)(2,1)S(1)}, u32[]{:S(2)}, u32[]{:S(2)}) collective-permute-start(bf16[256,2,1,256]{3,0,2,1:T(8,128)(2,1)} %get-tuple-element.221), channel_id=1, source_target_pairs={{0,8},{8,16},{16,24},{24,32},{32,40},{40,48},{48,56},{56,64},{64,7... | collective-permute-start | bytes 786440 | tf_op jit(solution)/shard_map/while/body/eval_jaxpr/ppermute | solution.py:15
  (49 other events, 430.8 us)
Sparse Core Ops, SparseCore 0:
  518.8 165.8 reduce-scatter.1
